TPU v7x, 128 devices: a whole 4x4x4 slice. The times are simulated.
128 devices in a mesh: dp: 4 (over x_lo, core), expert: 32 (over y, x_hi, z).
Axes of the slice: x: 4 (x_hi: 2, x_lo: 2; x = x_hi * 2 + x_lo), y: 4, z: 4, core: 2. Of those that a mesh axis runs over, the one named last changes fastest.
Arguments:
- hidden_in: bfloat16 [16384, 2048], P(('dp', 'expert')), may hold values from -6 to 6
- attn_gain: float32 [2048], replicated, may hold values from 0.1 to 1.9
- query_key_value_weight: bfloat16 [2048, 2560], P('expert'), may hold values from -0.125 to 0.125
- q_gain: float32 [128], replicated, may hold values from 0.1 to 1.9
- key_norm_gain: float32 [128], replicated, may hold values from 0.1 to 1.9
- w_out: bfloat16 [2048, 2048], P('expert'), may hold values from -0.125 to 0.125
- moe_gain: float32 [2048], replicated, may hold values from 0.1 to 1.9
- w_gate_up: bfloat16 [128, 2048, 1536], P(('dp', 'expert')), may hold values from -0.125 to 0.125
- w_down: bfloat16 [128, 768, 2048], P(('dp', 'expert')), may hold values from -0.21875 to 0.21875
- kv_pool: bfloat16 [32, 2, 128, 2, 128], P('dp'), may hold values from -160 to 160
- page_table: int32 [32], replicated, may hold values from 0 to 31, each once
- suffix_lengths: int32 [4, 4], replicated, may hold values from 1 to 2560, 4096 in all within a row
- request_group: int32 [4, 4], replicated, may hold values from 0 to 1
- expert_ids: int32 [16384, 8], P(('dp', 'expert')), may hold values from 0 to 127, all different within a row; in each aligned block of 128 rows (0 to 127, 128 to 255, ...) at most 12 rows name the same one
- gate_weights: float32 [16384, 8], P(('dp', 'expert')), may hold values from 0.05 to 0.3
Outputs:
- hidden_out: bfloat16 [16384, 2048], P(('dp', 'expert'))
- suffix_cache: bfloat16 [16384, 512], P(('dp', 'expert'))
Inputs may be any that keep to these rules, and one draw needn't show every extreme that they name: page_table holds each pool page once. `suffix_lengths`: each row sums to 4096; the largest of each row is exactly 2560. `expert_ids`: a token's 8 experts differ; among the 128 rows of one device no expert is named more than 12 times, and that many times in some device.
All inputs are finite; a program needn't handle non-finite values.
Results may differ from a plain program's by a relative error of at most 0.01.
The roundings to bfloat16 on the way count: a program that leaves them out, or rounds other values in their place, can miss the bound.
Values may be sent and summed in bfloat16 or wider, within the bound.
A program may use at most 256 MiB of HBM per device.

v0:
```python
import math
import jax
import jax.numpy as jnp
from jax import lax
from jax.sharding import PartitionSpec as P

PREFIX_TOKENS = 2048
PAGE_TOKENS = 128
eps = 1e-06
theta = 1000000.0
floor_value = -1e30


def root_mean_scale(value_rows, gain):
    value_rows = value_rows.astype(jnp.float32)
    return (
        value_rows
        * lax.rsqrt(jnp.mean(value_rows * value_rows, axis=-1, keepdims=True) + eps)
        * gain
    )


def rotary_apply(value_rows, token_positions):
    half = value_rows.shape[-1] // 2
    freqs = theta ** (-jnp.arange(half, dtype=jnp.float32) / half)
    angles = token_positions.astype(jnp.float32)[:, None] * freqs[None, :]
    cosine = jnp.cos(angles)[:, None, :]
    sine = jnp.sin(angles)[:, None, :]
    first = value_rows[..., :half]
    second_split = value_rows[..., half:]
    return jnp.concatenate(
        [first * cosine - second_split * sine, second_split * cosine + first * sine], axis=-1
    )


def layout(lengths_row, index):
    ends = jnp.cumsum(lengths_row)
    starts = ends - lengths_row
    request = jnp.sum((index[:, None] >= ends[None, :]).astype(jnp.int32), axis=1)
    chosen = request[:, None] == jnp.arange(lengths_row.shape[0], dtype=jnp.int32)[None, :]
    offset = index - jnp.sum(jnp.where(chosen, starts[None, :], 0), axis=1)
    return (request, offset, chosen)


def attend(carry, queries, key_rows, value_rows, mask, scale):
    high, total, acc = carry
    scores = (
        jnp.einsum("qkgd,skd->kgqs", queries, key_rows, preferred_element_type=jnp.float32) * scale
    )
    scores = jnp.where(mask[None, None], scores, -jnp.inf)
    new_high = jnp.maximum(high, jnp.max(scores, axis=-1))
    weights = jnp.exp(scores - new_high[..., None])
    scale_factor = jnp.exp(high - new_high)
    total = total * scale_factor + jnp.sum(weights, axis=-1)
    acc = acc * scale_factor[..., None] + jnp.einsum(
        "kgqs,skd->kgqd",
        weights.astype(jnp.bfloat16),
        value_rows,
        preferred_element_type=jnp.float32,
    )
    return (new_high, total, acc)


def expert_rows(rows, gate_up, down):
    both = jnp.dot(rows, gate_up, preferred_element_type=jnp.float32)
    half = both.shape[1] // 2
    act = (jax.nn.silu(both[:, :half]) * both[:, half:]).astype(jnp.bfloat16)
    return jnp.dot(act, down, preferred_element_type=jnp.float32).astype(jnp.bfloat16)


def local(
    hidden_in,
    attn_gain,
    query_key_value_weight,
    q_gain,
    key_norm_gain,
    w_out,
    moe_gain,
    w_gate_up,
    w_down,
    kv_pool,
    page_table,
    suffix_lengths,
    request_group,
    expert_ids,
    gate_weights,
):
    tokens_here, width = hidden_in.shape
    page_rows = kv_pool.shape[2]
    kv_heads = kv_pool.shape[3]
    head_dim = kv_pool.shape[4]
    key_value_width = kv_heads * head_dim
    query_width = query_key_value_weight.shape[1] - 2 * key_value_width
    q_heads = query_width // head_dim
    head_split = q_heads // kv_heads
    scale = 1.0 / math.sqrt(head_dim)
    row_count = lax.axis_size("dp")
    col_count = lax.axis_size("expert")
    row = lax.axis_index("dp")
    col = lax.axis_index("expert")
    normed = root_mean_scale(hidden_in, attn_gain).astype(jnp.bfloat16)
    part = normed
    qkv = jnp.dot(
        part,
        lax.all_gather(query_key_value_weight, "expert", axis=0, tiled=True),
        preferred_element_type=jnp.float32,
    )
    index = col * tokens_here + jnp.arange(tokens_here, dtype=jnp.int32)
    lengths_row = lax.dynamic_index_in_dim(suffix_lengths, row, 0, keepdims=False)
    groups_row = lax.dynamic_index_in_dim(request_group, row, 0, keepdims=False)
    request, offset, chosen = layout(lengths_row, index)
    qgroup = jnp.sum(jnp.where(chosen, groups_row[None, :], 0), axis=1)
    token_positions = PREFIX_TOKENS + offset
    queries = rotary_apply(
        root_mean_scale(qkv[:, :query_width].reshape(tokens_here, q_heads, head_dim), q_gain),
        token_positions,
    ).astype(jnp.bfloat16)
    key_rows = rotary_apply(
        root_mean_scale(
            qkv[:, query_width : query_width + key_value_width].reshape(
                tokens_here, kv_heads, head_dim
            ),
            key_norm_gain,
        ),
        token_positions,
    ).astype(jnp.bfloat16)
    value_rows = (
        qkv[:, query_width + key_value_width :]
        .reshape(tokens_here, kv_heads, head_dim)
        .astype(jnp.bfloat16)
    )
    suffix_cache = jnp.concatenate(
        [
            key_rows.reshape(tokens_here, key_value_width),
            value_rows.reshape(tokens_here, key_value_width),
        ],
        axis=1,
    )
    grouped = queries.reshape(tokens_here, kv_heads, head_split, head_dim)
    carry = (
        jnp.full((kv_heads, head_split, tokens_here), floor_value, jnp.float32),
        jnp.zeros((kv_heads, head_split, tokens_here), jnp.float32),
        jnp.zeros((kv_heads, head_split, tokens_here, head_dim), jnp.float32),
    )
    piece_keys = lax.all_gather(key_rows, "expert", axis=0, tiled=True)
    piece_values = lax.all_gather(value_rows, "expert", axis=0, tiled=True)
    key_index = jnp.arange(piece_keys.shape[0], dtype=jnp.int32)
    key_request, _, _ = layout(lengths_row, key_index)
    mask = (key_request[None, :] == request[:, None]) & (key_index[None, :] <= index[:, None])
    carry = attend(carry, grouped, piece_keys, piece_values, mask, scale)
    per_group = PREFIX_TOKENS // PAGE_TOKENS
    slot_ids = jnp.arange(page_table.shape[0], dtype=jnp.int32)
    piece = lax.all_gather(kv_pool, "dp", axis=0, tiled=True)
    count = piece.shape[0]
    hit = page_table[None, :] == jnp.arange(count, dtype=jnp.int32)[:, None]
    key_group = jnp.repeat(
        jnp.sum(jnp.where(hit, slot_ids[None, :] // per_group, 0), axis=1), page_rows
    )
    mask = key_group[None, :] == qgroup[:, None]
    carry = attend(
        carry,
        grouped,
        piece[:, 0].reshape(count * page_rows, kv_heads, head_dim),
        piece[:, 1].reshape(count * page_rows, kv_heads, head_dim),
        mask,
        scale,
    )
    mixed = (
        (carry[2] / carry[1][..., None])
        .transpose(2, 0, 1, 3)
        .reshape(tokens_here, query_width)
        .astype(jnp.bfloat16)
    )
    part = mixed
    projected = jnp.dot(
        part,
        lax.all_gather(w_out, "expert", axis=0, tiled=True),
        preferred_element_type=jnp.float32,
    )
    mid = (hidden_in.astype(jnp.float32) + projected).astype(jnp.bfloat16)
    moe_in = root_mean_scale(mid, moe_gain).astype(jnp.bfloat16)
    top_k = expert_ids.shape[1]
    expert_count = row_count * col_count
    capacity = max(2, tokens_here * top_k * 3 // (2 * expert_count))
    flat = expert_ids.reshape(-1)
    onehot = (flat[:, None] == jnp.arange(expert_count, dtype=jnp.int32)[None, :]).astype(jnp.int32)
    slot = jnp.sum((jnp.cumsum(onehot, axis=0) - onehot) * onehot, axis=1)
    place = flat * capacity + slot
    sources = jnp.repeat(moe_in, top_k, axis=0)
    outgoing = jnp.zeros((expert_count * capacity, width), jnp.bfloat16).at[place].set(sources)
    gate_up = w_gate_up[0]
    down = w_down[0]
    received = lax.all_to_all(
        outgoing.reshape(expert_count, capacity, width),
        ("dp", "expert"),
        split_axis=0,
        concat_axis=0,
        tiled=True,
    )
    results = expert_rows(received.reshape(-1, width), gate_up, down).reshape(received.shape)
    returned = lax.all_to_all(results, ("dp", "expert"), split_axis=0, concat_axis=0, tiled=True)
    picked = returned.reshape(expert_count * capacity, width)[place].astype(jnp.float32)
    moe = jnp.sum(picked.reshape(tokens_here, top_k, width) * gate_weights[:, :, None], axis=1)
    hidden_out = (mid.astype(jnp.float32) + moe).astype(jnp.bfloat16)
    return (hidden_out, suffix_cache)


def solution(mesh):
    return jax.shard_map(
        local,
        mesh=mesh,
        in_specs=(
            P(("dp", "expert"), None),
            P(),
            P("expert", None),
            P(),
            P(),
            P("expert", None),
            P(),
            P(("dp", "expert"), None, None),
            P(("dp", "expert"), None, None),
            P("dp", None, None, None, None),
            P(),
            P(),
            P(),
            P(("dp", "expert"), None),
            P(("dp", "expert"), None),
        ),
        out_specs=(P(("dp", "expert"), None), P(("dp", "expert"), None)),
        check_vma=False,
    )
```

profile of v0, /device:TPU:67, one launch (start us, length us, event | category | flops | bytes accessed | tf_op | source)
XLA Modules:
  0.0 756.2 jit_solution(2184994517330569896)
XLA Ops:
  8.0 2.6 copy.97
  14.0 114.5 %all-gather.6.cloned.1.call-done = bf16[2048,2560]{1,0:T(8,128)(2,1)} async-done(((bf16[64,2560]{1,0:T(8,128)(2,1)}), bf16[2048,2560]{1,0:T(8,128)(2,1)}) %all-gather.6.cloned.1.call-update) | async-done | bytes 10485776 | tf_op jit(solution)/shard_map/all_gather | solution.py:105
  128.5 5.7 fusion.68
  151.2 3.1 fusion.29
  154.3 21.2 %all-gather.12.cloned.1.call-done = bf16[32,2,128,2,128]{4,2,3,1,0:T(8,128)(2,1)} async-done(((bf16[8,2,128,2,128]{4,2,3,1,0:T(8,128)(2,1)}), bf16[32,2,128,2,128]{4,2,3,1,0:T(8,128)(2,1)}) %all-gather.12.cloned.1.call-update) | async-done | bytes 4194320 | tf_op jit(solution)/shard_map/all_gather | solution.py:153
  175.5 4.1 fusion.94
  181.2 4.6 copy.99
  185.8 4.2 reshape.374
  196.5 13.6 %bitcast_reduce_fusion = (f32[2,8,128]{2,1,0:T(8,128)S(1)}, f32[2,128,8,4096]{3,1,2,0:T(8,128)}) fusion(pred[128,4096]{1,0:T(8,128)(4,1)S(1)} %copy-done.2, bf16[4096,2,128,1]{2,0,3,1:T(8,128)(2,1)S(1)} %bitcast.168, bf16[128,2,8,64]{3,0,2,1:T(8,128)(2,1)S(1)} %bitcast.171, bf16[128,2,8,64]{3,0,2,1:T(8,128)(2,1)S(1)} %bitcast.169), kind=kOutput, calls=%fused_computation.3 | convolution fusion | flops 2173696000 | bytes 36708352 | tf_op jit(solution)/shard_map/qkgd,skd->kgqs/dot_general | solution.py:48
  210.1 38.8 %all-gather.8.cloned.1.call-done = bf16[4096,2,128]{2,0,1:T(8,128)(2,1)} async-done(((bf16[128,2,128]{2,0,1:T(8,128)(2,1)}), bf16[4096,2,128]{2,0,1:T(8,128)(2,1)}) %all-gather.8.cloned.1.call-update) | async-done | bytes 2097168 | tf_op jit(solution)/shard_map/all_gather | solution.py:145
  249.0 15.0 %fusion.3 = (f32[2,8,128]{2,1,0:T(8,128)S(1)}, f32[2,4096,128,8]{2,1,3,0:T(8,128)}) fusion(pred[128,4096]{0,1:T(8,128)(4,1)} %fusion.29, bf16[128,2,8,64]{3,0,2,1:T(8,128)(2,1)} %bitcast.172, bf16[128,2,8,64]{3,0,2,1:T(8,128)(2,1)} %bitcast.170, bf16[4096,2,128]{2,0,1:T(8,128)(2,1)} %all-gather.8.cloned.1.call-done), kind=kOutput, calls=%fused_computation.10 | convolution fusion | flops 2173696000 | bytes 36708352 | tf_op jit(solution)/shard_map/qkgd,skd->kgqs/dot_general | solution.py:48
  264.0 16.4 %fusion.1 = f32[2,8,128]{2,1,0:T(8,128)S(1)} fusion(f32[2,4096,128,8]{2,1,3,0:T(8,128)} %get-tuple-element.22, f32[2,8,128]{2,1,0:T(8,128)S(1)} %get-tuple-element.16, pred[128,4096]{0,1:T(8,128)(4,1)S(1)} %copy-done.4), kind=kLoop, calls=%fused_computation.8 | loop fusion | flops 33552384 | bytes 34095104 | tf_op jit(solution)/shard_map/reduce_sum | solution.py:54
  280.3 3.9 copy-done.1
  284.2 9.5 %fusion.4 = f32[2,8,128]{2,1,0:T(8,128)S(1)} fusion(f32[2,128,8,4096]{3,1,2,0:T(8,128)S(1)} %copy-done.1, f32[2,8,128]{2,1,0:T(8,128)S(1)} %get-tuple-element.15, pred[128,4096]{1,0:T(8,128)(4,1)S(1)} %copy-done.3), kind=kLoop, calls=%fused_computation.11 | loop fusion | flops 33552384 | bytes 34095104 | tf_op jit(solution)/shard_map/reduce_sum | solution.py:54
  293.8 28.9 %all-gather.10.cloned.1.call-done = bf16[4096,2,128]{0,2,1:T(8,128)(2,1)} async-done(((bf16[128,2,128]{0,2,1:T(8,128)(2,1)}), bf16[4096,2,128]{0,2,1:T(8,128)(2,1)}) %all-gather.10.cloned.1.call-update) | async-done | bytes 2097168 | tf_op jit(solution)/shard_map/all_gather | solution.py:146
  322.7 16.3 %fusion.50 = f32[128,2,8,128]{0,3,2,1:T(8,128)} fusion(f32[2,4096,128,8]{2,1,3,0:T(8,128)} %get-tuple-element.22, f32[2,8,128]{2,1,0:T(8,128)S(1)} %get-tuple-element.16, pred[128,4096]{0,1:T(8,128)(4,1)} %fusion.29, bf16[4096,2,128]{0,2,1:T(8,128)(2,1)} %all-gather.10.cloned.1.call-done, f32[128,2,8]{0,2,1:T(8,128)S(1)} %get-tuple-element.5, ...), kind=kOutput, calls=%fused_computation.45 | convolution fusion | flops 2181562368 | bytes 37249024 | tf_op jit(solution)/shard_map/kgqs,skd->kgqd/dot_general | solution.py:55
  339.0 16.3 %fusion.60 = bf16[128,2,8,128]{0,3,2,1:T(8,128)(2,1)} fusion(f32[128,2,8,128]{0,3,2,1:T(8,128)} %fusion.50, bf16[4096,2,128,1]{0,2,1,3:T(8,128)(2,1)} %reshape.374, f32[2,128,8,4096]{3,1,2,0:T(8,128)} %get-tuple-element.20, f32[2,8,128]{2,1,0:T(8,128)S(1)} %get-tuple-element.15, pred[128,4096]{1,0:T(8,128)(4,1)} %broadcast_compare_fusion, ...), kind=kOutput, calls=%fused_computation.47 | convolution fusion | flops 2181824512 | bytes 37765120 | tf_op jit(solution)/shard_map/kgqs,skd->kgqd/dot_general | solution.py:55
  355.4 73.6 %all-gather.14.cloned.1.call-done = bf16[2048,2048]{1,0:T(8,128)(2,1)} async-done(((bf16[64,2048]{1,0:T(8,128)(2,1)}), bf16[2048,2048]{1,0:T(8,128)(2,1)}) %all-gather.14.cloned.1.call-update) | async-done | bytes 8388624 | tf_op jit(solution)/shard_map/all_gather | solution.py:177
  429.0 4.9 multiply_reduce_fusion
  435.9 10.9 %scatter_custom_fusion = bf16[1536,2048]{1,0:T(8,128)(2,1)} fusion(s32[1024]{0:T(1024)S(1)} %bitcast.176, bf16[]{:T(256)} %constant.80.clone.1, bf16[128,2048]{1,0:T(8,128)(2,1)} %multiply_convert_fusion), kind=kCustom, calls=%fused_computation.24 | custom fusion | bytes 6815746 | tf_op jit(solution)/shard_map/scatter | solution.py:190
  446.8 10.6 %reshape.350 = bf16[128,12,2048]{2,1,0:T(8,128)(2,1)} reshape(bf16[1536,2048]{1,0:T(8,128)(2,1)} %scatter_custom_fusion) | data formatting | bytes 12582912 | tf_op jit(solution)/shard_map/reshape | solution.py:194
  457.4 105.0 %all_to_all.10 = bf16[128,12,2048]{2,1,0:T(8,128)(2,1)} all-to-all(bf16[128,12,2048]{2,1,0:T(8,128)(2,1)} %reshape.350), channel_id=1, replica_groups=mesh['dp'=4,'expert'=32] {'dp','expert'}, dimensions={0} | all-to-all | bytes 12582912 | tf_op jit(solution)/shard_map/all_to_all | solution.py:193
  562.4 10.7 %reshape.351 = bf16[1536,2048]{1,0:T(8,128)(2,1)} reshape(bf16[128,12,2048]{2,1,0:T(8,128)(2,1)} %all_to_all.10) | data formatting | bytes 12582912 | tf_op jit(solution)/shard_map/reshape | solution.py:200
  573.1 14.1 %fusion.13 = f32[1536,1536]{1,0:T(8,128)S(1)} fusion(bf16[1536,2048]{1,0:T(8,128)(2,1)} %reshape.351, bf16[1,2048,1536]{2,1,0:T(8,128)(2,1)} %param.22), kind=kOutput, calls=%fused_computation.20 | convolution fusion | flops 9663676416 | bytes 22020096 | tf_op jit(solution)/shard_map/dot_general | solution.py:65
  587.3 7.1 convolution_convert_fusion
  594.3 10.6 %reshape.352 = bf16[128,12,2048]{2,1,0:T(8,128)(2,1)} reshape(bf16[1536,2048]{1,0:T(8,128)(2,1)} %convolution_convert_fusion) | data formatting | bytes 12582912 | tf_op jit(solution)/shard_map/reshape | solution.py:200
  604.9 7.6 %all-to-all-start.1 = ((bf16[128,12,2048]{2,1,0:T(8,128)(2,1)}), bf16[128,12,2048]{2,1,0:T(8,128)(2,1)}, u32[]{:S(2)}, u32[]{:S(2)}) async-start(bf16[128,12,2048]{2,1,0:T(8,128)(2,1)} %reshape.352), calls=%async_computation.1 | async-start | bytes 16777216 | tf_op jit(solution)/shard_map/all_to_all | solution.py:201
  613.5 104.1 %all-to-all-done.1 = bf16[128,12,2048]{2,1,0:T(8,128)(2,1)} async-done(((bf16[128,12,2048]{2,1,0:T(8,128)(2,1)}), bf16[128,12,2048]{2,1,0:T(8,128)(2,1)}, u32[]{:S(2)}, u32[]{:S(2)}) %all-to-all-start.1) | async-done | bytes 6291488 | tf_op jit(solution)/shard_map/all_to_all | solution.py:201
  717.5 10.7 %reshape.353 = bf16[1536,2048]{1,0:T(8,128)(2,1)} reshape(bf16[128,12,2048]{2,1,0:T(8,128)(2,1)} %all-to-all-done.1) | data formatting | bytes 12582912 | tf_op jit(solution)/shard_map/reshape | solution.py:202
  728.2 12.4 %gather_fusion = bf16[1024,2048]{1,0:T(8,128)(2,1)} fusion(bf16[1536,2048]{1,0:T(8,128)(2,1)} %reshape.353, s32[1024]{0:T(1024)S(1)} %broadcast_clamp_fusion), kind=kCustom, calls=%fused_computation | custom fusion | bytes 8392704 | tf_op jit(solution)/shard_map/gather | solution.py:202
  740.7 6.5 fusion.12
  747.2 2.2 add_convert_fusion
  (117 shorter events, 31.9 us)
Async XLA Ops:
  7.2 580.1 %copy-start = (bf16[1,768,2048]{2,1,0:T(8,128)(2,1)S(1)}, bf16[1,768,2048]{2,1,0:T(8,128)(2,1)}, u32[]{:S(2)}) copy-start(bf16[1,768,2048]{2,1,0:T(8,128)(2,1)} %param.23) | copy-start | bytes 9437188
  7.2 121.3 %all-gather.6.cloned.1.call-start = ((), (), s32[]{:S(2)}) async-start(), calls=%async_computation.2 | async-start | bytes 10813440 | tf_op jit(solution)/shard_map/all_gather | solution.py:105
  7.9 167.6 %all-gather.12.cloned.1.call-start = ((), (), s32[]{:S(2)}) async-start(), calls=%async_computation.5 | async-start | bytes 5242880 | tf_op jit(solution)/shard_map/all_gather | solution.py:153
  10.6 238.4 %all-gather.8.cloned.1.call-start = ((), (), s32[]{:S(2)}) async-start(), calls=%async_computation.3 | async-start | bytes 2162688 | tf_op jit(solution)/shard_map/all_gather | solution.py:145
  14.0 124.9 %copy-start.21 = (f32[128]{0:T(128)S(1)}, f32[128]{0:T(128)}, u32[]{:S(2)}) copy-start(f32[128]{0:T(128)} %param.19) | copy-start | bytes 1540
  14.0 129.0 %copy-start.18 = (s32[128,8]{0,1:T(8,128)S(1)}, s32[128,8]{0,1:T(8,128)}, u32[]{:S(2)}) copy-start(s32[128,8]{0,1:T(8,128)} %param.28) | copy-start | bytes 12292
  14.0 132.2 %copy-start.23 = (s32[32]{0:T(128)S(1)}, s32[32]{0:T(128)}, u32[]{:S(2)}) copy-start(s32[32]{0:T(128)} %param.25) | copy-start | bytes 388
  134.3 1.1 copy-start.8
  139.1 0.6 copy-start.12
  139.1 0.6 copy-start.14
  140.5 182.2 %all-gather.10.cloned.1.call-start = ((), (), s32[]{:S(2)}) async-start(), calls=%async_computation.4 | async-start | bytes 2162688 | tf_op jit(solution)/shard_map/all_gather | solution.py:146
  141.5 1.4 copy-start.16
  142.2 286.7 %all-gather.14.cloned.1.call-start = ((), (), s32[]{:S(2)}) async-start(), calls=%async_computation.6 | async-start | bytes 8650752 | tf_op jit(solution)/shard_map/all_gather | solution.py:177
  143.5 0.8 copy-start.11
  179.5 13.5 %copy-start.22 = (f32[128]{0:T(128)S(1)}, f32[128]{0:T(128)}, u32[]{:S(2)}) copy-start(f32[128]{0:T(128)} %param.18) | copy-start | bytes 1540
  191.5 1.0 copy-start.6
  193.0 3.4 copy-start.2
  193.1 3.4 copy-start.7
  195.5 0.8 copy-start.9
  195.6 0.9 copy-start.10
  249.0 15.0 %copy-start.4 = (pred[128,4096]{0,1:T(8,128)(4,1)S(1)}, pred[128,4096]{0,1:T(8,128)(4,1)}, u32[]{:S(2)}) copy-start(pred[128,4096]{0,1:T(8,128)(4,1)} %fusion.29) | copy-start | bytes 1572868
  263.9 20.3 %copy-start.1 = (f32[2,128,8,4096]{3,1,2,0:T(8,128)S(1)}, f32[2,128,8,4096]{3,1,2,0:T(8,128)}, u32[]{:S(2)}) copy-start(f32[2,128,8,4096]{3,1,2,0:T(8,128)} %get-tuple-element.20) | copy-start | bytes 100663296
  264.0 20.3 %copy-start.3 = (pred[128,4096]{1,0:T(8,128)(4,1)S(1)}, pred[128,4096]{1,0:T(8,128)(4,1)}, u32[]{:S(2)}) copy-start(pred[128,4096]{1,0:T(8,128)(4,1)} %broadcast_compare_fusion) | copy-start | bytes 1572868
  429.0 6.0 copy-start.19
  433.9 1.0 copy-start.5
  604.9 7.7 %copy-start.20 = (f32[128,8]{0,1:T(8,128)S(1)}, f32[128,8]{0,1:T(8,128)}, u32[]{:S(2)}) copy-start(f32[128,8]{0,1:T(8,128)} %param.29) | copy-start | bytes 12292
  604.9 7.8 %copy-start.13 = (bf16[128,2,64]{2,0,1:T(8,128)(2,1)S(1)}, bf16[128,2,64]{2,0,1:T(8,128)(2,1)}, u32[]{:S(2)}) copy-start(bf16[128,2,64]{2,0,1:T(8,128)(2,1)} %copy-done.12) | copy-start | bytes 98308
  604.9 7.8 %copy-start.15 = (bf16[128,2,64]{2,0,1:T(8,128)(2,1)S(1)}, bf16[128,2,64]{2,0,1:T(8,128)(2,1)}, u32[]{:S(2)}) copy-start(bf16[128,2,64]{2,0,1:T(8,128)(2,1)} %copy-done.14) | copy-start | bytes 98308
  604.9 7.9 %copy-start.17 = (bf16[128,256]{1,0:T(8,128)(2,1)S(1)}, bf16[128,256]{1,0:T(8,128)(2,1)}, u32[]{:S(2)}) copy-start(bf16[128,256]{1,0:T(8,128)(2,1)} %copy-done.16) | copy-start | bytes 196612
  604.9 112.6 %all-to-all-start.1 = ((bf16[128,12,2048]{2,1,0:T(8,128)(2,1)}), bf16[128,12,2048]{2,1,0:T(8,128)(2,1)}, u32[]{:S(2)}, u32[]{:S(2)}) async-start(bf16[128,12,2048]{2,1,0:T(8,128)(2,1)} %reshape.352), calls=%async_computation.1 | async-start | bytes 16777216 | tf_op jit(solution)/shard_map/all_to_all | solution.py:201
Sparse Core Ops, SparseCore 0:
  11.1 117.4 all-gather.5
  130.2 45.2 all-gather.11
  179.3 69.6 all-gather.7
  251.6 71.0 all-gather.9
  325.6 103.2 all-gather.13
where the time goes:
time: 762 us; the launch traced here: 756 us
  waiting for transfers between devices  382 us (50%)
  blocking collectives  105 us (14%)
  local copies, waits for them, and re-layouts  102 us (13%)
  matrix products  93.2 us (12%)
  other arithmetic  51.6 us (7%)
  between operations  14.5 us (2%)
  starting transfers between devices  7.85 us (1%)
    all_gather x1, waiting for transfers between devices, local(): lax.all_gather(query_key_value_weight, 'expert', axis=0, tiled=True)  114 us
    all_to_all x1, blocking collectives, local(): lax.all_to_all(outgoing.reshape(expert_count, capacity, width), ('dp', 'e...  105 us
    all_to_all x1, waiting for transfers between devices, local(): lax.all_to_all(results, ('dp', 'expert'), split_axis=0, concat_axis=0, ti...  104 us
    all_gather x1, waiting for transfers between devices, local(): lax.all_gather(w_out, 'expert', axis=0, tiled=True)  73.6 us
    all_gather x1, waiting for transfers between devices, local(): piece_keys = lax.all_gather(key_rows, 'expert', axis=0, tiled=True)  38.8 us
    dot_general x2, matrix products, attend(): jnp.einsum('kgqs,skd->kgqd', weights.astype(jnp.bfloat16), value_rows, pr...  32.7 us
    all_gather x1, waiting for transfers between devices, local(): piece_values = lax.all_gather(value_rows, 'expert', axis=0, tiled=True)  28.9 us
    dot_general x2, matrix products, attend(): jnp.einsum('qkgd,skd->kgqs', queries, key_rows, preferred_element_type=jn...  28.6 us
  transfers between devices with their start and end apart: 6, of which 6 were waited for; matrix products, arithmetic and copies ran while one was open for 18% of the time, Pallas kernels for 0%

commit v1 on v0

--- a/solution.py
+++ b/solution.py
@@ -3,6 +3,7 @@
 import jax.numpy as jnp
 from jax import lax
 from jax.sharding import PartitionSpec as P
+from jax.lax import all_gather
 
 PREFIX_TOKENS = 2048
 PAGE_TOKENS = 128
@@ -142,8 +143,13 @@
         jnp.zeros((kv_heads, head_split, tokens_here), jnp.float32),
         jnp.zeros((kv_heads, head_split, tokens_here, head_dim), jnp.float32),
     )
-    piece_keys = lax.all_gather(key_rows, "expert", axis=0, tiled=True)
-    piece_values = lax.all_gather(value_rows, "expert", axis=0, tiled=True)
+    piece_keys, piece_values = jnp.split(
+        all_gather(
+            jnp.concatenate([key_rows, value_rows], axis=1), axis_name="expert", axis=0, tiled=True
+        ),
+        [key_rows.shape[1]],
+        axis=1,
+    )
     key_index = jnp.arange(piece_keys.shape[0], dtype=jnp.int32)
     key_request, _, _ = layout(lengths_row, key_index)
     mask = (key_request[None, :] == request[:, None]) & (key_index[None, :] <= index[:, None])

time: 762 us -> 698 us (0.916)
  waiting for transfers between devices: 382 us -> 318 us
    all_gather x1, waiting for transfers between devices: 73.6 us -> 27.9 us  [local(): lax.all_gather(w_out, 'expert', axis=0, tiled=True)]
    all_gather x2 -> x1, waiting for transfers between devices: 67.8 us -> 49.5 us  [local(): all_gather(jnp.concatenate([key_rows, value_rows], axis=1), axis_name='ex...]
  transfers between devices with their start and end apart: 6 -> 5, of which waited for: 6 -> 5; matrix products, arithmetic and copies ran while one was open for 18% -> 20% of each run, Pallas kernels for 0% -> 0%
where the time goes in v1:
time: 698 us; the launch traced here: 693 us
  waiting for transfers between devices  318 us (46%)
  blocking collectives  105 us (15%)
  local copies, waits for them, and re-layouts  102 us (15%)
  matrix products  93.6 us (13%)
  other arithmetic  51.6 us (7%)
  between operations  14.5 us (2%)
  starting transfers between devices  7.79 us (1%)
    all_gather x1, waiting for transfers between devices, local(): lax.all_gather(query_key_value_weight, 'expert', axis=0, tiled=True)  114 us
    all_to_all x1, blocking collectives, local(): lax.all_to_all(outgoing.reshape(expert_count, capacity, width), ('dp', 'e...  105 us
    all_to_all x1, waiting for transfers between devices, local(): lax.all_to_all(results, ('dp', 'expert'), split_axis=0, concat_axis=0, ti...  103 us
    all_gather x1, waiting for transfers between devices, local(): all_gather(jnp.concatenate([key_rows, value_rows], axis=1), axis_name='ex...  49.5 us
    dot_general x2, matrix products, attend(): jnp.einsum('kgqs,skd->kgqd', weights.astype(jnp.bfloat16), value_rows, pr...  33 us
    dot_general x2, matrix products, attend(): jnp.einsum('qkgd,skd->kgqs', queries, key_rows, preferred_element_type=jn...  28.8 us
    all_gather x1, waiting for transfers between devices, local(): lax.all_gather(w_out, 'expert', axis=0, tiled=True)  27.9 us
    reduce_sum x2, other arithmetic, attend(): total = total * scale_factor + jnp.sum(weights, axis=-1)  25.9 us
  transfers between devices with their start and end apart: 5, of which 5 were waited for; matrix products, arithmetic and copies ran while one was open for 20% of the time, Pallas kernels for 0%

profile of v1, /device:TPU:67, one launch (start us, length us, event | category | flops | bytes accessed | tf_op | source)
XLA Modules:
  0.0 692.7 jit_solution(10252315292533270627)
XLA Ops:
  8.0 2.7 copy.103
  14.1 114.4 %all-gather.5.cloned.1.call-done = bf16[2048,2560]{1,0:T(8,128)(2,1)} async-done(((bf16[64,2560]{1,0:T(8,128)(2,1)}), bf16[2048,2560]{1,0:T(8,128)(2,1)}) %all-gather.5.cloned.1.call-update) | async-done | bytes 10485776 | tf_op jit(solution)/shard_map/all_gather | solution.py:106
  128.5 5.7 fusion.60
  145.6 1.9 copy.110
  150.4 3.1 fusion.27
  153.5 22.0 %all-gather.9.cloned.1.call-done = bf16[32,2,128,2,128]{4,2,3,1,0:T(8,128)(2,1)} async-done(((bf16[8,2,128,2,128]{4,2,3,1,0:T(8,128)(2,1)}), bf16[32,2,128,2,128]{4,2,3,1,0:T(8,128)(2,1)}) %all-gather.9.cloned.1.call-update) | async-done | bytes 4194320 | tf_op jit(solution)/shard_map/all_gather | solution.py:159
  175.5 4.1 fusion.86
  181.2 4.6 copy.105
  185.8 4.2 reshape.374
  196.5 13.7 %bitcast_reduce_fusion = (f32[2,8,128]{2,1,0:T(8,128)S(1)}, f32[2,128,8,4096]{3,1,2,0:T(8,128)}) fusion(pred[128,4096]{1,0:T(8,128)(4,1)S(1)} %copy-done.2, bf16[4096,2,128,1]{2,0,3,1:T(8,128)(2,1)S(1)} %bitcast.172, bf16[128,2,8,64]{3,0,2,1:T(8,128)(2,1)S(1)} %bitcast.175, bf16[128,2,8,64]{3,0,2,1:T(8,128)(2,1)S(1)} %bitcast.173), kind=kOutput, calls=%fused_computation.3 | convolution fusion | flops 2173696000 | bytes 36708352 | tf_op jit(solution)/shard_map/qkgd,skd->kgqs/dot_general | solution.py:49
  210.1 49.5 %all-gather.7.cloned.1.call-done = bf16[4096,4,128]{2,0,1:T(8,128)(2,1)} async-done(((bf16[128,4,128]{2,0,1:T(8,128)(2,1)}), bf16[4096,4,128]{2,0,1:T(8,128)(2,1)}) %all-gather.7.cloned.1.call-update) | async-done | bytes 4194320 | tf_op jit(solution)/shard_map/all_gather | solution.py:147
  259.7 15.1 %fusion.3 = (f32[2,8,128]{2,1,0:T(8,128)S(1)}, f32[2,4096,128,8]{2,1,3,0:T(8,128)}) fusion(pred[128,4096]{0,1:T(8,128)(4,1)} %fusion.27, bf16[128,2,8,64]{3,0,2,1:T(8,128)(2,1)} %bitcast.176, bf16[128,2,8,64]{3,0,2,1:T(8,128)(2,1)} %bitcast.174, bf16[4096,4,128]{2,0,1:T(8,128)(2,1)} %all-gather.7.cloned.1.call-done), kind=kOutput, calls=%fused_computation.10 | convolution fusion | flops 2173696000 | bytes 37232640 | tf_op jit(solution)/shard_map/qkgd,skd->kgqs/dot_general | solution.py:49
  274.8 16.4 %fusion.1 = f32[2,8,128]{2,1,0:T(8,128)S(1)} fusion(f32[2,4096,128,8]{2,1,3,0:T(8,128)} %get-tuple-element.22, f32[2,8,128]{2,1,0:T(8,128)S(1)} %get-tuple-element.16, pred[128,4096]{0,1:T(8,128)(4,1)S(1)} %copy-done.9), kind=kLoop, calls=%fused_computation.8 | loop fusion | flops 33552384 | bytes 34095104 | tf_op jit(solution)/shard_map/reduce_sum | solution.py:55
  291.2 3.9 copy-done.1
  295.1 9.5 %fusion.4 = f32[2,8,128]{2,1,0:T(8,128)S(1)} fusion(f32[2,128,8,4096]{3,1,2,0:T(8,128)S(1)} %copy-done.1, f32[2,8,128]{2,1,0:T(8,128)S(1)} %get-tuple-element.15, pred[128,4096]{1,0:T(8,128)(4,1)S(1)} %copy-done.3), kind=kLoop, calls=%fused_computation.11 | loop fusion | flops 33552384 | bytes 34095104 | tf_op jit(solution)/shard_map/reduce_sum | solution.py:55
  304.7 16.4 %fusion.44 = f32[128,2,8,128]{0,3,2,1:T(8,128)} fusion(bf16[4096,4,128]{2,0,1:T(8,128)(2,1)} %all-gather.7.cloned.1.call-done, f32[2,4096,128,8]{2,1,3,0:T(8,128)} %get-tuple-element.22, f32[2,8,128]{2,1,0:T(8,128)S(1)} %get-tuple-element.16, pred[128,4096]{0,1:T(8,128)(4,1)} %fusion.27, f32[128,2,8]{0,2,1:T(8,128)S(1)} %get-tuple-element.5, ...), kind=kOutput, calls=%fused_computation.45 | convolution fusion | flops 2181562368 | bytes 37249024 | tf_op jit(solution)/shard_map/kgqs,skd->kgqd/dot_general | solution.py:56
  321.1 16.6 %fusion.52 = bf16[128,2,8,128]{0,3,2,1:T(8,128)(2,1)} fusion(f32[128,2,8,128]{0,3,2,1:T(8,128)} %fusion.44, bf16[4096,2,128,1]{0,2,1,3:T(8,128)(2,1)} %reshape.374, f32[2,128,8,4096]{3,1,2,0:T(8,128)} %get-tuple-element.20, f32[2,8,128]{2,1,0:T(8,128)S(1)} %get-tuple-element.15, pred[128,4096]{1,0:T(8,128)(4,1)} %broadcast_compare_fusion, ...), kind=kOutput, calls=%fused_computation.47 | convolution fusion | flops 2181824512 | bytes 37765120 | tf_op jit(solution)/shard_map/kgqs,skd->kgqd/dot_general | solution.py:56
  337.6 27.9 %all-gather.11.cloned.1.call-done = bf16[2048,2048]{1,0:T(8,128)(2,1)} async-done(((bf16[64,2048]{1,0:T(8,128)(2,1)}), bf16[2048,2048]{1,0:T(8,128)(2,1)}) %all-gather.11.cloned.1.call-update) | async-done | bytes 8388624 | tf_op jit(solution)/shard_map/all_gather | solution.py:183
  365.5 4.9 multiply_reduce_fusion
  372.4 10.9 %scatter_custom_fusion = bf16[1536,2048]{1,0:T(8,128)(2,1)} fusion(s32[1024]{0:T(1024)S(1)} %bitcast.179, bf16[]{:T(256)} %constant.80.clone.1, bf16[128,2048]{1,0:T(8,128)(2,1)} %multiply_convert_fusion), kind=kCustom, calls=%fused_computation.24 | custom fusion | bytes 6815746 | tf_op jit(solution)/shard_map/scatter | solution.py:196
  383.3 10.6 %reshape.350 = bf16[128,12,2048]{2,1,0:T(8,128)(2,1)} reshape(bf16[1536,2048]{1,0:T(8,128)(2,1)} %scatter_custom_fusion) | data formatting | bytes 12582912 | tf_op jit(solution)/shard_map/reshape | solution.py:200
  393.9 105.0 %all_to_all.10 = bf16[128,12,2048]{2,1,0:T(8,128)(2,1)} all-to-all(bf16[128,12,2048]{2,1,0:T(8,128)(2,1)} %reshape.350), channel_id=1, replica_groups=mesh['dp'=4,'expert'=32] {'dp','expert'}, dimensions={0} | all-to-all | bytes 12582912 | tf_op jit(solution)/shard_map/all_to_all | solution.py:199
  498.9 10.7 %reshape.351 = bf16[1536,2048]{1,0:T(8,128)(2,1)} reshape(bf16[128,12,2048]{2,1,0:T(8,128)(2,1)} %all_to_all.10) | data formatting | bytes 12582912 | tf_op jit(solution)/shard_map/reshape | solution.py:206
  509.6 14.1 %fusion.13 = f32[1536,1536]{1,0:T(8,128)S(1)} fusion(bf16[1536,2048]{1,0:T(8,128)(2,1)} %reshape.351, bf16[1,2048,1536]{2,1,0:T(8,128)(2,1)} %param.22), kind=kOutput, calls=%fused_computation.20 | convolution fusion | flops 9663676416 | bytes 22020096 | tf_op jit(solution)/shard_map/dot_general | solution.py:66
  523.8 7.1 %convolution_convert_fusion = bf16[1536,2048]{1,0:T(8,128)(2,1)} fusion(bf16[1,768,2048]{2,1,0:T(8,128)(2,1)S(1)} %copy-done, f32[1536,1536]{1,0:T(8,128)S(1)} %fusion.13), kind=kOutput, calls=%fused_computation.19 | convolution fusion | flops 4842061824 | bytes 18874368 | tf_op jit(solution)/shard_map/dot_general | solution.py:69
  530.9 10.6 %reshape.352 = bf16[128,12,2048]{2,1,0:T(8,128)(2,1)} reshape(bf16[1536,2048]{1,0:T(8,128)(2,1)} %convolution_convert_fusion) | data formatting | bytes 12582912 | tf_op jit(solution)/shard_map/reshape | solution.py:206
  541.4 7.6 %all-to-all-start.1 = ((bf16[128,12,2048]{2,1,0:T(8,128)(2,1)}), bf16[128,12,2048]{2,1,0:T(8,128)(2,1)}, u32[]{:S(2)}, u32[]{:S(2)}) async-start(bf16[128,12,2048]{2,1,0:T(8,128)(2,1)} %reshape.352), calls=%async_computation.1 | async-start | bytes 16777216 | tf_op jit(solution)/shard_map/all_to_all | solution.py:207
  550.9 103.2 %all-to-all-done.1 = bf16[128,12,2048]{2,1,0:T(8,128)(2,1)} async-done(((bf16[128,12,2048]{2,1,0:T(8,128)(2,1)}), bf16[128,12,2048]{2,1,0:T(8,128)(2,1)}, u32[]{:S(2)}, u32[]{:S(2)}) %all-to-all-start.1) | async-done | bytes 6291488 | tf_op jit(solution)/shard_map/all_to_all | solution.py:207
  654.1 10.7 %reshape.353 = bf16[1536,2048]{1,0:T(8,128)(2,1)} reshape(bf16[128,12,2048]{2,1,0:T(8,128)(2,1)} %all-to-all-done.1) | data formatting | bytes 12582912 | tf_op jit(solution)/shard_map/reshape | solution.py:208
  664.8 12.4 %gather_fusion = bf16[1024,2048]{1,0:T(8,128)(2,1)} fusion(bf16[1536,2048]{1,0:T(8,128)(2,1)} %reshape.353, s32[1024]{0:T(1024)S(1)} %broadcast_clamp_fusion), kind=kCustom, calls=%fused_computation | custom fusion | bytes 8392704 | tf_op jit(solution)/shard_map/gather | solution.py:208
  677.2 6.5 fusion.12
  683.7 2.2 add_convert_fusion
  (111 shorter events, 29.9 us)
Async XLA Ops:
  7.2 516.6 %copy-start = (bf16[1,768,2048]{2,1,0:T(8,128)(2,1)S(1)}, bf16[1,768,2048]{2,1,0:T(8,128)(2,1)}, u32[]{:S(2)}) copy-start(bf16[1,768,2048]{2,1,0:T(8,128)(2,1)} %param.23) | copy-start | bytes 9437188
  7.2 121.3 %all-gather.5.cloned.1.call-start = ((), (), s32[]{:S(2)}) async-start(), calls=%async_computation.2 | async-start | bytes 10813440 | tf_op jit(solution)/shard_map/all_gather | solution.py:106
  7.9 167.6 %all-gather.9.cloned.1.call-start = ((), (), s32[]{:S(2)}) async-start(), calls=%async_computation.4 | async-start | bytes 5242880 | tf_op jit(solution)/shard_map/all_gather | solution.py:159
  10.7 249.0 %all-gather.7.cloned.1.call-start = ((), (), s32[]{:S(2)}) async-start(), calls=%async_computation.3 | async-start | bytes 4325376 | tf_op jit(solution)/shard_map/all_gather | solution.py:147
  14.1 124.8 %copy-start.19 = (f32[128]{0:T(128)S(1)}, f32[128]{0:T(128)}, u32[]{:S(2)}) copy-start(f32[128]{0:T(128)} %param.19) | copy-start | bytes 1540
  14.1 128.1 %copy-start.16 = (s32[128,8]{0,1:T(8,128)S(1)}, s32[128,8]{0,1:T(8,128)}, u32[]{:S(2)}) copy-start(s32[128,8]{0,1:T(8,128)} %param.28) | copy-start | bytes 12292
  14.1 131.3 %copy-start.21 = (s32[32]{0:T(128)S(1)}, s32[32]{0:T(128)}, u32[]{:S(2)}) copy-start(s32[32]{0:T(128)} %param.25) | copy-start | bytes 388
  134.3 1.1 copy-start.7
  139.1 0.6 copy-start.12
  139.1 0.7 copy-start.14
  141.5 224.0 %all-gather.11.cloned.1.call-start = ((), (), s32[]{:S(2)}) async-start(), calls=%async_computation.5 | async-start | bytes 8650752 | tf_op jit(solution)/shard_map/all_gather | solution.py:183
  142.7 0.8 copy-start.8
  181.2 11.9 %copy-start.20 = (f32[128]{0:T(128)S(1)}, f32[128]{0:T(128)}, u32[]{:S(2)}) copy-start(f32[128]{0:T(128)} %param.18) | copy-start | bytes 1540
  191.5 1.0 copy-start.5
  193.1 3.4 copy-start.2
  193.1 3.4 copy-start.6
  195.5 0.8 copy-start.10
  195.6 0.8 copy-start.11
  259.7 15.1 %copy-start.9 = (pred[128,4096]{0,1:T(8,128)(4,1)S(1)}, pred[128,4096]{0,1:T(8,128)(4,1)}, u32[]{:S(2)}) copy-start(pred[128,4096]{0,1:T(8,128)(4,1)} %fusion.27) | copy-start | bytes 1572868
  274.8 20.3 %copy-start.1 = (f32[2,128,8,4096]{3,1,2,0:T(8,128)S(1)}, f32[2,128,8,4096]{3,1,2,0:T(8,128)}, u32[]{:S(2)}) copy-start(f32[2,128,8,4096]{3,1,2,0:T(8,128)} %get-tuple-element.20) | copy-start | bytes 100663296
  274.8 20.3 %copy-start.3 = (pred[128,4096]{1,0:T(8,128)(4,1)S(1)}, pred[128,4096]{1,0:T(8,128)(4,1)}, u32[]{:S(2)}) copy-start(pred[128,4096]{1,0:T(8,128)(4,1)} %broadcast_compare_fusion) | copy-start | bytes 1572868
  365.5 6.0 copy-start.17
  370.5 1.0 copy-start.4
  541.4 7.6 %copy-start.18 = (f32[128,8]{0,1:T(8,128)S(1)}, f32[128,8]{0,1:T(8,128)}, u32[]{:S(2)}) copy-start(f32[128,8]{0,1:T(8,128)} %param.29) | copy-start | bytes 12292
  541.4 8.7 %copy-start.13 = (bf16[128,2,64]{2,0,1:T(8,128)(2,1)S(1)}, bf16[128,2,64]{2,0,1:T(8,128)(2,1)}, u32[]{:S(2)}) copy-start(bf16[128,2,64]{2,0,1:T(8,128)(2,1)} %copy-done.12) | copy-start | bytes 98308
  541.4 8.7 %copy-start.15 = (bf16[128,2,64]{2,0,1:T(8,128)(2,1)S(1)}, bf16[128,2,64]{2,0,1:T(8,128)(2,1)}, u32[]{:S(2)}) copy-start(bf16[128,2,64]{2,0,1:T(8,128)(2,1)} %copy-done.14) | copy-start | bytes 98308
  541.4 112.6 %all-to-all-start.1 = ((bf16[128,12,2048]{2,1,0:T(8,128)(2,1)}), bf16[128,12,2048]{2,1,0:T(8,128)(2,1)}, u32[]{:S(2)}, u32[]{:S(2)}) async-start(bf16[128,12,2048]{2,1,0:T(8,128)(2,1)} %reshape.352), calls=%async_computation.1 | async-start | bytes 16777216 | tf_op jit(solution)/shard_map/all_to_all | solution.py:207
Sparse Core Ops, SparseCore 0:
  11.1 117.4 all-gather.4
  130.2 45.2 all-gather.8
  179.3 80.3 all-gather.6
  262.6 102.8 all-gather.10
